TPU v7x, 32 devices: a whole 2x2x4 slice. The times are simulated.
32 devices in a mesh: groups: 2 (over y), shard: 16 (over z, x, core).
Axes of the slice: x: 2, y: 2, z: 4, core: 2. Of those that a mesh axis runs over, the one named last changes fastest.
Arguments:
- query_tokens: bfloat16 [1024, 32, 128], P(('groups', 'shard')), parts along dimension 0, may hold values from -0.1875 to 0.1875
- candidates: int32 [1024, 24], P(('groups', 'shard')), parts along dimension 0, may hold values from 0 to 511, as said below
- cand_count: int32 [1024], P(('groups', 'shard')), parts along dimension 0, may hold values from 3 to 24, as said below
- placement_map: int32 [1024], P('groups'), parts along dimension 0, may hold values from 0 to 511, as said below
- passage_base: bfloat16 [1024, 128, 128], P(('groups', 'shard')), parts along dimension 0, may hold values from -6 to 6
- residual_codes: int32 [1024, 128, 128], P(('groups', 'shard')), parts along dimension 0, may hold values from 0 to 3
- passage_lengths: int32 [1024], P(('groups', 'shard')), parts along dimension 0, may hold values from 32 to 128
- bucket_weights: float32 [8], P('groups'), parts along dimension 0, may hold values from -3 to 3
Outputs:
- scores: float32 [1024, 24], P(('groups', 'shard')), parts along dimension 0
There are 2 independent parts, one for each index of `groups`. A program takes and returns all parts, laid end to end along the dimension named above; each array names one. Nothing has to cross between parts.
Inputs may be any that keep to these rules, and one draw needn't show every extreme that they name: In row q the first cand_count[q] entries are distinct passage ids; the devices that store them (device placement_map[id] // 32 of the shard axis) are at most 3, and one device stores at most 8 of them. Of the 32 queries of one device, one storing device (the same for all devices) holds candidates of exactly 9, and every other storing device holds candidates of at most 6. Entries at or beyond cand_count[q] are arbitrary ids. `cand_count`: entries of candidates at or beyond this count are not scored. A permutation: passage id p is row placement_map[p] of the passage store.
All inputs are finite; a program needn't handle non-finite values.
Results may differ from a plain program's by a relative error of at most 0.0003.
Values may be sent and summed in bfloat16 or wider, within the bound.
A program may use at most 64 MiB of HBM per device.

v0:
```python
import jax
import jax.numpy as jnp
from jax import lax
from jax.sharding import PartitionSpec as P

OWNERS_Q = 3
CPQ = 8
epsilon = 1e-06
negative = -1e30


def decode(bases, code_ids, levels):
    residual = jnp.zeros(bases.shape, jnp.float32)
    for bucket in range(4):
        residual = residual + jnp.where(code_ids == bucket, levels[bucket], 0.0)
    summed = bases.astype(jnp.float32) + residual
    inverse_norm = lax.rsqrt(jnp.sum(summed * summed, axis=-1, keepdims=True) + epsilon)
    return (summed * inverse_norm).astype(jnp.bfloat16)


def score_block(query_rows, token_rows, lengths):
    similarity_scores = jnp.einsum(
        "mqd,mkpd->mqkp", query_rows, token_rows, preferred_element_type=jnp.float32
    )
    inside = (
        jnp.arange(token_rows.shape[2], dtype=jnp.int32)[None, None, None, :]
        < lengths[:, None, :, None]
    )
    maxima = jnp.max(jnp.where(inside, similarity_scores, negative), axis=3)
    return jnp.sum(maxima, axis=1)


def score_slots(query_rows, wanted, decoded, lengths):
    item_count = query_rows.shape[0]
    group_size = 16
    padding = -item_count % group_size
    wanted = jnp.maximum(wanted, 0)
    blocks = (item_count + padding) // group_size

    def one_block(bundle):
        query_part, row_part = bundle
        return score_block(query_part, decoded[row_part], lengths[row_part])

    result = lax.map(
        one_block,
        (
            query_rows.reshape(blocks, group_size, query_rows.shape[1], query_rows.shape[2]),
            wanted.reshape(blocks, group_size, wanted.shape[1]),
        ),
    )
    return result.reshape(blocks * group_size, wanted.shape[1])


def pack(present, holder, capacity, query_tokens):
    present_int = present.astype(jnp.int32)
    slot_of = jnp.cumsum(present_int, axis=0) - present_int
    selection_mask = present.T[:, None, :] & (
        slot_of.T[:, None, :] == jnp.arange(capacity, dtype=jnp.int32)[None, :, None]
    )
    outgoing = jnp.einsum(
        "ksq,qtd->kstd",
        selection_mask.astype(jnp.bfloat16),
        query_tokens,
        preferred_element_type=jnp.float32,
    ).astype(jnp.bfloat16)
    target = (
        jnp.sum(
            selection_mask[:, :, :, None].astype(jnp.int32)
            * (jnp.transpose(holder, (1, 0, 2))[:, None, :, :] + 1),
            axis=2,
        )
        - 1
    )
    return (outgoing, target, slot_of)


def local(
    query_tokens,
    candidates,
    cand_count,
    placement_map,
    passage_base,
    residual_codes,
    passage_lengths,
    bucket_weights,
):
    device_count = lax.axis_size("shard")
    query_count, slot_count = candidates.shape
    store_rows = passage_base.shape[0]
    hot_cap = query_count * OWNERS_Q // device_count + 3
    decoded = decode(passage_base, residual_codes, bucket_weights)
    usable = jnp.arange(slot_count, dtype=jnp.int32)[None, :] < cand_count[:, None]
    stored = placement_map[candidates]
    holders = stored // store_rows
    local_row = stored % store_rows
    shared = usable[:, :, None] & usable[:, None, :] & (holders[:, :, None] == holders[:, None, :])
    preceding_total = (
        jnp.arange(slot_count, dtype=jnp.int32)[None, :]
        < jnp.arange(slot_count, dtype=jnp.int32)[:, None]
    )
    within = jnp.sum((shared & preceding_total[None, :, :]).astype(jnp.int32), axis=2)
    owner_ids = jnp.arange(device_count, dtype=jnp.int32)
    matches = usable[:, :, None] & (holders[:, :, None] == owner_ids[None, None, :])
    present = jnp.any(matches, axis=1)
    rank_ids = jnp.arange(CPQ, dtype=jnp.int32)
    holder = (
        jnp.sum(
            jnp.where(
                matches[:, :, :, None]
                & (within[:, :, None, None] == rank_ids[None, None, None, :]),
                local_row[:, :, None, None] + 1,
                0,
            ),
            axis=1,
        )
        - 1
    )
    outgoing, target, slot_of = pack(present, holder, hot_cap, query_tokens)
    queries_in = lax.all_to_all(outgoing, "shard", split_axis=0, concat_axis=0, tiled=True)
    rows_in = lax.all_to_all(
        target.astype(jnp.bfloat16), "shard", split_axis=0, concat_axis=0, tiled=True
    )
    senders = rows_in.shape[0]
    slots_in = rows_in.shape[1]
    flat_queries = queries_in.reshape(senders * slots_in, queries_in.shape[2], queries_in.shape[3])
    row_list_flat = rows_in.astype(jnp.int32).reshape(senders * slots_in, rows_in.shape[2])
    visited = score_slots(flat_queries, row_list_flat, decoded, passage_lengths).reshape(
        senders, slots_in, rows_in.shape[2]
    )
    returned = lax.all_to_all(visited, "shard", split_axis=0, concat_axis=0, tiled=True)
    flattened = returned.reshape(-1)
    pick_slot = jnp.take_along_axis(slot_of, jnp.clip(holders, 0, device_count - 1), axis=1)
    position = holders * (hot_cap * CPQ) + pick_slot * CPQ + within
    result = jnp.take(flattened, position, mode="clip")
    return jnp.where(usable, result, 0.0)


def solution(mesh):
    return jax.shard_map(
        local,
        mesh=mesh,
        in_specs=(
            P(("groups", "shard"), None, None),
            P(("groups", "shard"), None),
            P(("groups", "shard")),
            P("groups"),
            P(("groups", "shard"), None, None),
            P(("groups", "shard"), None, None),
            P(("groups", "shard")),
            P("groups"),
        ),
        out_specs=P(("groups", "shard"), None),
        check_vma=False,
    )
```

profile of v0, /device:TPU:0, one launch (start us, length us, event | category | flops | bytes accessed | tf_op | source)
XLA Modules:
  0.0 154.1 jit_solution(14491903596649840008)
XLA Ops:
  1.8 5.0 %gather_fusion.2 = s32[768]{0:T(1024)S(1)} fusion(s32[512]{0:T(512)S(1)} %copy-done, s32[1024]{0:T(1024)S(1)} %pad_clamp_fusion.2), kind=kCustom, calls=%fused_computation.2 | custom fusion | bytes 9216 | tf_op jit(solution)/shard_map/gather | solution.py:93
  11.2 7.4 %all-to-all-start = ((bf16[16,9,8]{1,2,0:T(8,128)(2,1)}), bf16[16,9,8]{1,2,0:T(8,128)(2,1)S(1)}, u32[]{:S(2)}, u32[]{:S(2)}) async-start(bf16[16,9,8]{1,2,0:T(8,128)(2,1)} %copy.114), calls=%async_computation | async-start | bytes 65536 | tf_op jit(solution)/shard_map/all_to_all | solution.py:120
  20.4 4.9 %all-to-all-done = bf16[16,9,8]{1,2,0:T(8,128)(2,1)S(1)} async-done(((bf16[16,9,8]{1,2,0:T(8,128)(2,1)}), bf16[16,9,8]{1,2,0:T(8,128)(2,1)S(1)}, u32[]{:S(2)}, u32[]{:S(2)}) %all-to-all-start) | async-done | bytes 2336 | tf_op jit(solution)/shard_map/all_to_all | solution.py:120
  25.2 4.4 %all-to-all-start.1 = ((bf16[16,9,32,128]{3,2,1,0:T(8,128)(2,1)}), bf16[16,9,32,128]{3,2,1,0:T(8,128)(2,1)}, u32[]{:S(2)}, u32[]{:S(2)}) async-start(bf16[16,9,32,128]{3,2,1,0:T(8,128)(2,1)} %copy.118), calls=%async_computation.1 | async-start | bytes 2359296 | tf_op jit(solution)/shard_map/all_to_all | solution.py:119
  30.0 5.1 %gather_fusion.4 = s32[768]{0:T(1024)S(1)} fusion(s32[32,16]{1,0:T(8,128)S(1)} %convert_subtract_fusion, s32[768]{0:T(1024)S(1)} %reshape.292), kind=kCustom, calls=%fused_computation.4 | custom fusion | bytes 12288 | tf_op jit(solution)/shard_map/jit(take_along_axis)/gather | solution.py:132
  36.2 4.8 %multiply_reduce_fusion = f32[32,128]{1,0:T(8,128)S(1)} fusion(f32[]{:T(128)} %bitcast.17, s32[32,128,128]{2,1,0:T(8,128)S(1)} %copy-done.2, f32[]{:T(128)} %bitcast.16, f32[]{:T(128)} %bitcast.15, f32[]{:T(128)} %bitcast.14, bf16[32,128,128]{2,1,0:T(8,128)(2,1)} %param.14), kind=kLoop, calls=%fused_computation.14 | loop fusion | flops 7860224 | bytes 3162128 | tf_op jit(solution)/shard_map/reduce_sum | solution.py:17
  41.0 4.6 %multiply_convert_fusion = bf16[32,128,128]{2,1,0:T(8,128)(2,1)S(1)} fusion(f32[32,128]{1,0:T(8,128)S(1)} %add_rsqrt_fusion, f32[]{:T(128)} %bitcast.17, s32[32,128,128]{2,1,0:T(8,128)S(1)} %copy-done.2, f32[]{:T(128)} %bitcast.16, f32[]{:T(128)} %bitcast.15, f32[]{:T(128)} %bitcast.14, bf16[32,128,128]{2,1,0:T(8,128)(2,1)} %param.14), kind=kLoop, calls=%fused_computation.13 | loop fusion | flops 7864320 | bytes 4210704 | tf_op jit(solution)/shard_map/convert_element_type | solution.py:18
  46.0 8.7 %all-to-all-done.1 = bf16[16,9,32,128]{3,2,1,0:T(8,128)(2,1)} async-done(((bf16[16,9,32,128]{3,2,1,0:T(8,128)(2,1)}), bf16[16,9,32,128]{3,2,1,0:T(8,128)(2,1)}, u32[]{:S(2)}, u32[]{:S(2)}) %all-to-all-start.1) | async-done | bytes 1179680 | tf_op jit(solution)/shard_map/all_to_all | solution.py:119
  54.7 78.7 %while.10 = (s32[]{:T(128)}, f32[9,16,8]{1,0,2:T(8,128)S(1)}, s32[9,16,8]{1,0,2:T(8,128)S(1)}, s32[32]{0:T(128)S(1)}, bf16[9,16,32,128]{3,2,1,0:T(8,128)(2,1)}, ...) while((s32[]{:T(128)}, f32[9,16,8]{1,0,2:T(8,128)S(1)}, ...), condition=%wide.region_9.10_spmd, body=%wide.region_6.9_spmd.sunk | while | flops 135283968 | bytes 12794485 | solution.py:44
  59.3 3.9 %select_reduce_fusion.3 = f32[16,32,8]{1,2,0:T(8,128)S(1)} fusion(bf16[16,8,128,128]{3,2,1,0:T(8,128)(2,1)} %bitcast.55, pred[16,8,128]{2,1,0:T(8,128)(4,1)S(1)} %iota_compare_fusion.7, bf16[9,16,32,128]{3,2,1,0:T(8,128)(2,1)} %get-tuple-element.147, s32[]{:T(128)S(6)} %copy.149), kind=kOutput, calls=%fused_computation.5.clone.1 | convolution fusion | flops 135262208 | bytes 4358148 | tf_op jit(solution)/shard_map/while/body/eval_jaxpr/mqd,mkpd->mqkp/dot_general | solution.py:22
  68.1 3.9 %select_reduce_fusion.3 = f32[16,32,8]{1,2,0:T(8,128)S(1)} fusion(bf16[16,8,128,128]{3,2,1,0:T(8,128)(2,1)} %bitcast.55, pred[16,8,128]{2,1,0:T(8,128)(4,1)S(1)} %iota_compare_fusion.7, bf16[9,16,32,128]{3,2,1,0:T(8,128)(2,1)} %get-tuple-element.147, s32[]{:T(128)S(6)} %copy.149), kind=kOutput, calls=%fused_computation.5.clone.1 | convolution fusion | flops 135262208 | bytes 4358148 | tf_op jit(solution)/shard_map/while/body/eval_jaxpr/mqd,mkpd->mqkp/dot_general | solution.py:22
  73.8 3.0 %gather_fusion = bf16[128,128,128]{2,1,0:T(8,128)(2,1)} fusion(bf16[32,128,128]{2,1,0:T(8,128)(2,1)S(1)} %get-tuple-element.148, s32[1024]{0:T(1024)S(1)} %pad_clamp_fusion.4), kind=kCustom, calls=%fused_computation.1.clone.1 | custom fusion | bytes 8389120 | tf_op jit(solution)/shard_map/while/body/eval_jaxpr/gather | solution.py:42
  76.8 3.9 %select_reduce_fusion.3 = f32[16,32,8]{1,2,0:T(8,128)S(1)} fusion(bf16[16,8,128,128]{3,2,1,0:T(8,128)(2,1)} %bitcast.55, pred[16,8,128]{2,1,0:T(8,128)(4,1)S(1)} %iota_compare_fusion.7, bf16[9,16,32,128]{3,2,1,0:T(8,128)(2,1)} %get-tuple-element.147, s32[]{:T(128)S(6)} %copy.149), kind=kOutput, calls=%fused_computation.5.clone.1 | convolution fusion | flops 135262208 | bytes 4358148 | tf_op jit(solution)/shard_map/while/body/eval_jaxpr/mqd,mkpd->mqkp/dot_general | solution.py:22
  85.6 3.9 %select_reduce_fusion.3 = f32[16,32,8]{1,2,0:T(8,128)S(1)} fusion(bf16[16,8,128,128]{3,2,1,0:T(8,128)(2,1)} %bitcast.55, pred[16,8,128]{2,1,0:T(8,128)(4,1)S(1)} %iota_compare_fusion.7, bf16[9,16,32,128]{3,2,1,0:T(8,128)(2,1)} %get-tuple-element.147, s32[]{:T(128)S(6)} %copy.149), kind=kOutput, calls=%fused_computation.5.clone.1 | convolution fusion | flops 135262208 | bytes 4358148 | tf_op jit(solution)/shard_map/while/body/eval_jaxpr/mqd,mkpd->mqkp/dot_general | solution.py:22
  94.3 3.9 %select_reduce_fusion.3 = f32[16,32,8]{1,2,0:T(8,128)S(1)} fusion(bf16[16,8,128,128]{3,2,1,0:T(8,128)(2,1)} %bitcast.55, pred[16,8,128]{2,1,0:T(8,128)(4,1)S(1)} %iota_compare_fusion.7, bf16[9,16,32,128]{3,2,1,0:T(8,128)(2,1)} %get-tuple-element.147, s32[]{:T(128)S(6)} %copy.149), kind=kOutput, calls=%fused_computation.5.clone.1 | convolution fusion | flops 135262208 | bytes 4358148 | tf_op jit(solution)/shard_map/while/body/eval_jaxpr/mqd,mkpd->mqkp/dot_general | solution.py:22
  100.0 3.0 %gather_fusion = bf16[128,128,128]{2,1,0:T(8,128)(2,1)} fusion(bf16[32,128,128]{2,1,0:T(8,128)(2,1)S(1)} %get-tuple-element.148, s32[1024]{0:T(1024)S(1)} %pad_clamp_fusion.4), kind=kCustom, calls=%fused_computation.1.clone.1 | custom fusion | bytes 8389120 | tf_op jit(solution)/shard_map/while/body/eval_jaxpr/gather | solution.py:42
  103.1 3.9 %select_reduce_fusion.3 = f32[16,32,8]{1,2,0:T(8,128)S(1)} fusion(bf16[16,8,128,128]{3,2,1,0:T(8,128)(2,1)} %bitcast.55, pred[16,8,128]{2,1,0:T(8,128)(4,1)S(1)} %iota_compare_fusion.7, bf16[9,16,32,128]{3,2,1,0:T(8,128)(2,1)} %get-tuple-element.147, s32[]{:T(128)S(6)} %copy.149), kind=kOutput, calls=%fused_computation.5.clone.1 | convolution fusion | flops 135262208 | bytes 4358148 | tf_op jit(solution)/shard_map/while/body/eval_jaxpr/mqd,mkpd->mqkp/dot_general | solution.py:22
  111.8 3.9 %select_reduce_fusion.3 = f32[16,32,8]{1,2,0:T(8,128)S(1)} fusion(bf16[16,8,128,128]{3,2,1,0:T(8,128)(2,1)} %bitcast.55, pred[16,8,128]{2,1,0:T(8,128)(4,1)S(1)} %iota_compare_fusion.7, bf16[9,16,32,128]{3,2,1,0:T(8,128)(2,1)} %get-tuple-element.147, s32[]{:T(128)S(6)} %copy.149), kind=kOutput, calls=%fused_computation.5.clone.1 | convolution fusion | flops 135262208 | bytes 4358148 | tf_op jit(solution)/shard_map/while/body/eval_jaxpr/mqd,mkpd->mqkp/dot_general | solution.py:22
  120.6 3.9 %select_reduce_fusion.3 = f32[16,32,8]{1,2,0:T(8,128)S(1)} fusion(bf16[16,8,128,128]{3,2,1,0:T(8,128)(2,1)} %bitcast.55, pred[16,8,128]{2,1,0:T(8,128)(4,1)S(1)} %iota_compare_fusion.7, bf16[9,16,32,128]{3,2,1,0:T(8,128)(2,1)} %get-tuple-element.147, s32[]{:T(128)S(6)} %copy.149), kind=kOutput, calls=%fused_computation.5.clone.1 | convolution fusion | flops 135262208 | bytes 4358148 | tf_op jit(solution)/shard_map/while/body/eval_jaxpr/mqd,mkpd->mqkp/dot_general | solution.py:22
  126.3 3.0 %gather_fusion = bf16[128,128,128]{2,1,0:T(8,128)(2,1)} fusion(bf16[32,128,128]{2,1,0:T(8,128)(2,1)S(1)} %get-tuple-element.148, s32[1024]{0:T(1024)S(1)} %pad_clamp_fusion.4), kind=kCustom, calls=%fused_computation.1.clone.1 | custom fusion | bytes 8389120 | tf_op jit(solution)/shard_map/while/body/eval_jaxpr/gather | solution.py:42
  129.3 3.9 %select_reduce_fusion.3 = f32[16,32,8]{1,2,0:T(8,128)S(1)} fusion(bf16[16,8,128,128]{3,2,1,0:T(8,128)(2,1)} %bitcast.55, pred[16,8,128]{2,1,0:T(8,128)(4,1)S(1)} %iota_compare_fusion.7, bf16[9,16,32,128]{3,2,1,0:T(8,128)(2,1)} %get-tuple-element.147, s32[]{:T(128)S(6)} %copy.149), kind=kOutput, calls=%fused_computation.5.clone.1 | convolution fusion | flops 135262208 | bytes 4358148 | tf_op jit(solution)/shard_map/while/body/eval_jaxpr/mqd,mkpd->mqkp/dot_general | solution.py:22
  134.2 7.4 %all-to-all-start.2 = ((f32[16,9,8]{1,2,0:T(8,128)}), f32[16,9,8]{1,2,0:T(8,128)S(1)}, u32[]{:S(2)}, u32[]{:S(2)}) async-start(f32[16,9,8]{1,2,0:T(8,128)} %copy.121), calls=%async_computation.2 | async-start | bytes 131072 | tf_op jit(solution)/shard_map/all_to_all | solution.py:130
  141.6 6.9 %all-to-all-done.2 = f32[16,9,8]{1,2,0:T(8,128)S(1)} async-done(((f32[16,9,8]{1,2,0:T(8,128)}), f32[16,9,8]{1,2,0:T(8,128)S(1)}, u32[]{:S(2)}, u32[]{:S(2)}) %all-to-all-start.2) | async-done | bytes 4640 | tf_op jit(solution)/shard_map/all_to_all | solution.py:130
  148.7 4.5 %gather_fusion.3 = f32[768]{0:T(1024)S(1)} fusion(f32[1152]{0:T(1024)S(1)} %reshape.259, s32[1024]{0:T(1024)S(1)} %pad_clamp_fusion.1), kind=kCustom, calls=%fused_computation.3 | custom fusion | bytes 9216 | tf_op jit(solution)/shard_map/jit(_take)/gather | solution.py:134
  (170 shorter events, 45.4 us)
Async XLA Ops:
  0.0 1.7 %copy-start = (s32[512]{0:T(512)S(1)}, s32[512]{0:T(512)}, u32[]{:S(2)}) copy-start(s32[512]{0:T(512)} %param.13) | copy-start | bytes 6148
  1.7 16.9 %copy-start.3 = (bf16[32,32,128]{2,1,0:T(8,128)(2,1)S(1)}, bf16[32,32,128]{2,1,0:T(8,128)(2,1)}, u32[]{:S(2)}) copy-start(bf16[32,32,128]{2,1,0:T(8,128)(2,1)} %param.10) | copy-start | bytes 786436
  11.2 14.0 %all-to-all-start = ((bf16[16,9,8]{1,2,0:T(8,128)(2,1)}), bf16[16,9,8]{1,2,0:T(8,128)(2,1)S(1)}, u32[]{:S(2)}, u32[]{:S(2)}) async-start(bf16[16,9,8]{1,2,0:T(8,128)(2,1)} %copy.114), calls=%async_computation | async-start | bytes 65536 | tf_op jit(solution)/shard_map/all_to_all | solution.py:120
  25.2 29.5 %all-to-all-start.1 = ((bf16[16,9,32,128]{3,2,1,0:T(8,128)(2,1)}), bf16[16,9,32,128]{3,2,1,0:T(8,128)(2,1)}, u32[]{:S(2)}, u32[]{:S(2)}) async-start(bf16[16,9,32,128]{3,2,1,0:T(8,128)(2,1)} %copy.118), calls=%async_computation.1 | async-start | bytes 2359296 | tf_op jit(solution)/shard_map/all_to_all | solution.py:119
  30.0 5.5 %copy-start.4 = (f32[4]{0:T(128)S(1)}, f32[4]{0:T(128)}, u32[]{:S(2)}) copy-start(f32[4]{0:T(128)} %param.17) | copy-start | bytes 52
  30.0 6.2 %copy-start.2 = (s32[32,128,128]{2,1,0:T(8,128)S(1)}, s32[32,128,128]{2,1,0:T(8,128)}, u32[]{:S(2)}) copy-start(s32[32,128,128]{2,1,0:T(8,128)} %param.15) | copy-start | bytes 6291460
  41.0 13.7 %copy-start.1 = (s32[32]{0:T(128)S(1)}, s32[32]{0:T(128)}, u32[]{:S(2)}) copy-start(s32[32]{0:T(128)} %param.16) | copy-start | bytes 388
  134.2 14.3 %all-to-all-start.2 = ((f32[16,9,8]{1,2,0:T(8,128)}), f32[16,9,8]{1,2,0:T(8,128)S(1)}, u32[]{:S(2)}, u32[]{:S(2)}) async-start(f32[16,9,8]{1,2,0:T(8,128)} %copy.121), calls=%async_computation.2 | async-start | bytes 131072 | tf_op jit(solution)/shard_map/all_to_all | solution.py:130
  148.7 4.6 %copy-start.5 = (s32[32]{0:T(128)S(1)}, s32[32]{0:T(128)}, u32[]{:S(2)}) copy-start(s32[32]{0:T(128)} %param.12) | copy-start | bytes 388
where the time goes:
time: 155 us; the launch traced here: 154 us
  local copies, waits for them, and re-layouts  62 us (40%)
  matrix products  35.5 us (23%)
  waiting for transfers between devices  20.4 us (13%)
  starting transfers between devices  19.2 us (12%)
  other arithmetic  16 us (10%)
    gather x27, local copies, waits for them, and re-layouts, one_block(): return score_block(query_part, decoded[row_part], lengths[row_part])  38.8 us
    dot_general x9, matrix products, score_block(): jnp.einsum('mqd,mkpd->mqkp', query_rows, token_rows, preferred_element_ty...  35 us
    all_to_all x1, waiting for transfers between devices, local(): lax.all_to_all(outgoing, 'shard', split_axis=0, concat_axis=0, tiled=True)  8.68 us
    all_to_all x1, starting transfers between devices, local(): lax.all_to_all(visited, 'shard', split_axis=0, concat_axis=0, tiled=True)  7.39 us
    all_to_all x1, starting transfers between devices, local(): lax.all_to_all(target.astype(jnp.bfloat16), 'shard', split_axis=0, concat...  7.39 us
    all_to_all x1, waiting for transfers between devices, local(): lax.all_to_all(visited, 'shard', split_axis=0, concat_axis=0, tiled=True)  6.88 us
    gather x5, local copies, waits for them, and re-layouts, local(): jnp.take_along_axis(slot_of, jnp.clip(holders, 0, device_count - 1), axis=1)  5.46 us
    gather x5, local copies, waits for them, and re-layouts, local(): stored = placement_map[candidates]  5.3 us
  transfers between devices with their start and end apart: 3, of which 3 were waited for; matrix products, arithmetic and copies ran while one was open for 12% of the time, Pallas kernels for 0%

commit v1 on v0

--- a/solution.py
+++ b/solution.py
@@ -7,6 +7,18 @@
 CPQ = 8
 epsilon = 1e-06
 negative = -1e30
+
+
+def rotated_exchange(array, axis, split, join):
+    ways, here = (lax.axis_size(axis), lax.axis_index(axis))
+    width = array.shape[split] // ways
+    turned = jnp.roll(array, -here * width, axis=split)
+    got = [lax.slice_in_dim(turned, 0, width, axis=split)]
+    for far in range(1, ways):
+        sent = lax.slice_in_dim(turned, far * width, (far + 1) * width, axis=split)
+        got.append(lax.ppermute(sent, axis, [(d, (d + far) % ways) for d in range(ways)]))
+    line = jnp.concatenate(got[::-1], axis=join)
+    return jnp.roll(line, (here + 1) * got[0].shape[join], axis=join)
 
 
 def decode(bases, code_ids, levels):
@@ -117,9 +129,7 @@
     )
     outgoing, target, slot_of = pack(present, holder, hot_cap, query_tokens)
     queries_in = lax.all_to_all(outgoing, "shard", split_axis=0, concat_axis=0, tiled=True)
-    rows_in = lax.all_to_all(
-        target.astype(jnp.bfloat16), "shard", split_axis=0, concat_axis=0, tiled=True
-    )
+    rows_in = rotated_exchange(target.astype(jnp.bfloat16), "shard", 0, 0)
     senders = rows_in.shape[0]
     slots_in = rows_in.shape[1]
     flat_queries = queries_in.reshape(senders * slots_in, queries_in.shape[2], queries_in.shape[3])

time: 155 us -> 160 us (1.032)
  starting transfers between devices: 19.2 us -> 36.1 us
  waiting for transfers between devices: 20.4 us -> 8.37 us
    ppermute x0 -> x15, starting transfers between devices: none -> 22.8 us  [rotated_exchange(): lax.ppermute(sent, axis, [(d, (d + far) % ways) for d in range(ways)])]
    all_to_all x1, waiting for transfers between devices: 8.68 us -> 0.01 us  [local(): lax.all_to_all(outgoing, 'shard', split_axis=0, concat_axis=0, tiled=True)]
    all_to_all x1 -> x0, starting transfers between devices: 7.39 us -> none  [local(): lax.all_to_all(target.astype(jnp.bfloat16), 'shard', split_axis=0, concat...]
    all_to_all x1 -> x0, waiting for transfers between devices: 4.85 us -> none  [local(): lax.all_to_all(target.astype(jnp.bfloat16), 'shard', split_axis=0, concat...]
    all_to_all x1, starting transfers between devices: 4.39 us -> 7.43 us  [local(): lax.all_to_all(outgoing, 'shard', split_axis=0, concat_axis=0, tiled=True)]
  transfers between devices with their start and end apart: 3 -> 17, of which waited for: 3 -> 3; matrix products, arithmetic and copies ran while one was open for 12% -> 13% of each run, Pallas kernels for 0% -> 0%
where the time goes in v1:
time: 160 us; the launch traced here: 159 us
  local copies, waits for them, and re-layouts  62.3 us (39%)
  starting transfers between devices  36.1 us (23%)
  matrix products  35.5 us (22%)
  other arithmetic  16.1 us (10%)
  waiting for transfers between devices  8.37 us (5%)
    gather x27, local copies, waits for them, and re-layouts, one_block(): return score_block(query_part, decoded[row_part], lengths[row_part])  39 us
    dot_general x9, matrix products, score_block(): jnp.einsum('mqd,mkpd->mqkp', query_rows, token_rows, preferred_element_ty...  35 us
    ppermute x15, starting transfers between devices, rotated_exchange(): lax.ppermute(sent, axis, [(d, (d + far) % ways) for d in range(ways)])  22.8 us
    all_to_all x1, starting transfers between devices, local(): lax.all_to_all(outgoing, 'shard', split_axis=0, concat_axis=0, tiled=True)  7.43 us
    all_to_all x1, waiting for transfers between devices, local(): lax.all_to_all(visited, 'shard', split_axis=0, concat_axis=0, tiled=True)  6.88 us
    all_to_all x1, starting transfers between devices, local(): lax.all_to_all(visited, 'shard', split_axis=0, concat_axis=0, tiled=True)  5.8 us
    gather x5, local copies, waits for them, and re-layouts, local(): jnp.take_along_axis(slot_of, jnp.clip(holders, 0, device_count - 1), axis=1)  5.46 us
    gather x5, local copies, waits for them, and re-layouts, local(): stored = placement_map[candidates]  5.3 us
  transfers between devices with their start and end apart: 17, of which 3 were waited for; matrix products, arithmetic and copies ran while one was open for 13% of the time, Pallas kernels for 0%

profile of v1, /device:TPU:0, one launch (start us, length us, event | category | flops | bytes accessed | tf_op | source)
XLA Modules:
  0.0 159.4 jit_solution(14190725806485052736)
XLA Ops:
  1.8 5.0 %gather_fusion.2 = s32[768]{0:T(1024)S(1)} fusion(s32[512]{0:T(512)S(1)} %copy-done, s32[1024]{0:T(1024)S(1)} %pad_clamp_fusion.2), kind=kCustom, calls=%fused_computation.2 | custom fusion | bytes 9216 | tf_op jit(solution)/shard_map/gather | solution.py:105
  9.0 7.4 %all-to-all-start = ((bf16[16,9,32,128]{3,2,1,0:T(8,128)(2,1)}), bf16[16,9,32,128]{3,2,1,0:T(8,128)(2,1)}, u32[]{:S(2)}, u32[]{:S(2)}) async-start(bf16[16,9,32,128]{3,2,1,0:T(8,128)(2,1)} %copy.117), calls=%async_computation | async-start | bytes 2359296 | tf_op jit(solution)/shard_map/all_to_all | solution.py:131
  26.9 5.1 %gather_fusion.4 = s32[768]{0:T(1024)S(1)} fusion(s32[32,16]{1,0:T(8,128)S(1)} %convert_subtract_fusion, s32[768]{0:T(1024)S(1)} %reshape.292), kind=kCustom, calls=%fused_computation.4 | custom fusion | bytes 12288 | tf_op jit(solution)/shard_map/jit(take_along_axis)/gather | solution.py:142
  33.0 4.8 %multiply_reduce_fusion = f32[32,128]{1,0:T(8,128)S(1)} fusion(f32[]{:T(128)} %bitcast.17, s32[32,128,128]{2,1,0:T(8,128)S(1)} %copy-done.2, f32[]{:T(128)} %bitcast.16, f32[]{:T(128)} %bitcast.15, f32[]{:T(128)} %bitcast.14, bf16[32,128,128]{2,1,0:T(8,128)(2,1)} %param.16), kind=kLoop, calls=%fused_computation.14 | loop fusion | flops 7860224 | bytes 3162128 | tf_op jit(solution)/shard_map/reduce_sum | solution.py:29
  37.7 4.6 %multiply_convert_fusion = bf16[32,128,128]{2,1,0:T(8,128)(2,1)S(1)} fusion(f32[32,128]{1,0:T(8,128)S(1)} %add_rsqrt_fusion, f32[]{:T(128)} %bitcast.17, s32[32,128,128]{2,1,0:T(8,128)S(1)} %copy-done.2, f32[]{:T(128)} %bitcast.16, f32[]{:T(128)} %bitcast.15, f32[]{:T(128)} %bitcast.14, bf16[32,128,128]{2,1,0:T(8,128)(2,1)} %param.16), kind=kLoop, calls=%fused_computation.13 | loop fusion | flops 7864320 | bytes 4210704 | tf_op jit(solution)/shard_map/convert_element_type | solution.py:30
  43.9 4.1 %collective-permute-start.8 = (bf16[1,9,8]{0,2,1:T(8,128)(2,1)S(1)}, bf16[1,9,8]{0,2,1:T(8,128)(2,1)S(1)}, u32[]{:S(2)}, u32[]{:S(2)}) collective-permute-start(bf16[1,9,8]{0,2,1:T(8,128)(2,1)S(1)} %get-tuple-element.88), channel_id=1, source_target_pairs={{0,7},{1,8},{2,9},{3,10},{4,11},{5,12},{6,13},{7,14},{8,15},{9,0},... | collective-permute-start | bytes 440 | tf_op jit(solution)/shard_map/ppermute | solution.py:19
  61.5 78.9 %while.10 = (s32[]{:T(128)}, f32[9,16,8]{1,0,2:T(8,128)S(1)}, s32[9,16,8]{1,0,2:T(8,128)S(1)}, s32[32]{0:T(128)S(1)}, bf16[9,16,32,128]{3,2,1,0:T(8,128)(2,1)}, ...) while((s32[]{:T(128)}, f32[9,16,8]{1,0,2:T(8,128)S(1)}, ...), condition=%wide.region_9.11_spmd, body=%wide.region_6.10_spmd.sunk | while | flops 135283968 | bytes 12794485 | solution.py:56
  63.1 3.0 %gather_fusion = bf16[128,128,128]{2,1,0:T(8,128)(2,1)} fusion(bf16[32,128,128]{2,1,0:T(8,128)(2,1)S(1)} %get-tuple-element.165, s32[1024]{0:T(1024)S(1)} %pad_clamp_fusion.4), kind=kCustom, calls=%fused_computation.1.clone.1 | custom fusion | bytes 8389120 | tf_op jit(solution)/shard_map/while/body/eval_jaxpr/gather | solution.py:54
  66.1 3.9 %select_reduce_fusion.3 = f32[16,32,8]{1,2,0:T(8,128)S(1)} fusion(bf16[16,8,128,128]{3,2,1,0:T(8,128)(2,1)} %bitcast.55, pred[16,8,128]{2,1,0:T(8,128)(4,1)S(1)} %iota_compare_fusion.7, bf16[9,16,32,128]{3,2,1,0:T(8,128)(2,1)} %get-tuple-element.164, s32[]{:T(128)S(6)} %copy.148), kind=kOutput, calls=%fused_computation.5.clone.1 | convolution fusion | flops 135262208 | bytes 4358148 | tf_op jit(solution)/shard_map/while/body/eval_jaxpr/mqd,mkpd->mqkp/dot_general | solution.py:34
  74.9 3.9 %select_reduce_fusion.3 = f32[16,32,8]{1,2,0:T(8,128)S(1)} fusion(bf16[16,8,128,128]{3,2,1,0:T(8,128)(2,1)} %bitcast.55, pred[16,8,128]{2,1,0:T(8,128)(4,1)S(1)} %iota_compare_fusion.7, bf16[9,16,32,128]{3,2,1,0:T(8,128)(2,1)} %get-tuple-element.164, s32[]{:T(128)S(6)} %copy.148), kind=kOutput, calls=%fused_computation.5.clone.1 | convolution fusion | flops 135262208 | bytes 4358148 | tf_op jit(solution)/shard_map/while/body/eval_jaxpr/mqd,mkpd->mqkp/dot_general | solution.py:34
  80.7 3.0 %gather_fusion = bf16[128,128,128]{2,1,0:T(8,128)(2,1)} fusion(bf16[32,128,128]{2,1,0:T(8,128)(2,1)S(1)} %get-tuple-element.165, s32[1024]{0:T(1024)S(1)} %pad_clamp_fusion.4), kind=kCustom, calls=%fused_computation.1.clone.1 | custom fusion | bytes 8389120 | tf_op jit(solution)/shard_map/while/body/eval_jaxpr/gather | solution.py:54
  83.7 3.9 %select_reduce_fusion.3 = f32[16,32,8]{1,2,0:T(8,128)S(1)} fusion(bf16[16,8,128,128]{3,2,1,0:T(8,128)(2,1)} %bitcast.55, pred[16,8,128]{2,1,0:T(8,128)(4,1)S(1)} %iota_compare_fusion.7, bf16[9,16,32,128]{3,2,1,0:T(8,128)(2,1)} %get-tuple-element.164, s32[]{:T(128)S(6)} %copy.148), kind=kOutput, calls=%fused_computation.5.clone.1 | convolution fusion | flops 135262208 | bytes 4358148 | tf_op jit(solution)/shard_map/while/body/eval_jaxpr/mqd,mkpd->mqkp/dot_general | solution.py:34
  89.4 3.0 %gather_fusion = bf16[128,128,128]{2,1,0:T(8,128)(2,1)} fusion(bf16[32,128,128]{2,1,0:T(8,128)(2,1)S(1)} %get-tuple-element.165, s32[1024]{0:T(1024)S(1)} %pad_clamp_fusion.4), kind=kCustom, calls=%fused_computation.1.clone.1 | custom fusion | bytes 8389120 | tf_op jit(solution)/shard_map/while/body/eval_jaxpr/gather | solution.py:54
  92.4 3.9 %select_reduce_fusion.3 = f32[16,32,8]{1,2,0:T(8,128)S(1)} fusion(bf16[16,8,128,128]{3,2,1,0:T(8,128)(2,1)} %bitcast.55, pred[16,8,128]{2,1,0:T(8,128)(4,1)S(1)} %iota_compare_fusion.7, bf16[9,16,32,128]{3,2,1,0:T(8,128)(2,1)} %get-tuple-element.164, s32[]{:T(128)S(6)} %copy.148), kind=kOutput, calls=%fused_computation.5.clone.1 | convolution fusion | flops 135262208 | bytes 4358148 | tf_op jit(solution)/shard_map/while/body/eval_jaxpr/mqd,mkpd->mqkp/dot_general | solution.py:34
  101.2 3.9 %select_reduce_fusion.3 = f32[16,32,8]{1,2,0:T(8,128)S(1)} fusion(bf16[16,8,128,128]{3,2,1,0:T(8,128)(2,1)} %bitcast.55, pred[16,8,128]{2,1,0:T(8,128)(4,1)S(1)} %iota_compare_fusion.7, bf16[9,16,32,128]{3,2,1,0:T(8,128)(2,1)} %get-tuple-element.164, s32[]{:T(128)S(6)} %copy.148), kind=kOutput, calls=%fused_computation.5.clone.1 | convolution fusion | flops 135262208 | bytes 4358148 | tf_op jit(solution)/shard_map/while/body/eval_jaxpr/mqd,mkpd->mqkp/dot_general | solution.py:34
  110.0 3.9 %select_reduce_fusion.3 = f32[16,32,8]{1,2,0:T(8,128)S(1)} fusion(bf16[16,8,128,128]{3,2,1,0:T(8,128)(2,1)} %bitcast.55, pred[16,8,128]{2,1,0:T(8,128)(4,1)S(1)} %iota_compare_fusion.7, bf16[9,16,32,128]{3,2,1,0:T(8,128)(2,1)} %get-tuple-element.164, s32[]{:T(128)S(6)} %copy.148), kind=kOutput, calls=%fused_computation.5.clone.1 | convolution fusion | flops 135262208 | bytes 4358148 | tf_op jit(solution)/shard_map/while/body/eval_jaxpr/mqd,mkpd->mqkp/dot_general | solution.py:34
  118.7 3.9 %select_reduce_fusion.3 = f32[16,32,8]{1,2,0:T(8,128)S(1)} fusion(bf16[16,8,128,128]{3,2,1,0:T(8,128)(2,1)} %bitcast.55, pred[16,8,128]{2,1,0:T(8,128)(4,1)S(1)} %iota_compare_fusion.7, bf16[9,16,32,128]{3,2,1,0:T(8,128)(2,1)} %get-tuple-element.164, s32[]{:T(128)S(6)} %copy.148), kind=kOutput, calls=%fused_computation.5.clone.1 | convolution fusion | flops 135262208 | bytes 4358148 | tf_op jit(solution)/shard_map/while/body/eval_jaxpr/mqd,mkpd->mqkp/dot_general | solution.py:34
  124.5 3.0 %gather_fusion = bf16[128,128,128]{2,1,0:T(8,128)(2,1)} fusion(bf16[32,128,128]{2,1,0:T(8,128)(2,1)S(1)} %get-tuple-element.165, s32[1024]{0:T(1024)S(1)} %pad_clamp_fusion.4), kind=kCustom, calls=%fused_computation.1.clone.1 | custom fusion | bytes 8389120 | tf_op jit(solution)/shard_map/while/body/eval_jaxpr/gather | solution.py:54
  127.5 3.9 %select_reduce_fusion.3 = f32[16,32,8]{1,2,0:T(8,128)S(1)} fusion(bf16[16,8,128,128]{3,2,1,0:T(8,128)(2,1)} %bitcast.55, pred[16,8,128]{2,1,0:T(8,128)(4,1)S(1)} %iota_compare_fusion.7, bf16[9,16,32,128]{3,2,1,0:T(8,128)(2,1)} %get-tuple-element.164, s32[]{:T(128)S(6)} %copy.148), kind=kOutput, calls=%fused_computation.5.clone.1 | convolution fusion | flops 135262208 | bytes 4358148 | tf_op jit(solution)/shard_map/while/body/eval_jaxpr/mqd,mkpd->mqkp/dot_general | solution.py:34
  133.2 3.0 %gather_fusion = bf16[128,128,128]{2,1,0:T(8,128)(2,1)} fusion(bf16[32,128,128]{2,1,0:T(8,128)(2,1)S(1)} %get-tuple-element.165, s32[1024]{0:T(1024)S(1)} %pad_clamp_fusion.4), kind=kCustom, calls=%fused_computation.1.clone.1 | custom fusion | bytes 8389120 | tf_op jit(solution)/shard_map/while/body/eval_jaxpr/gather | solution.py:54
  136.3 3.9 %select_reduce_fusion.3 = f32[16,32,8]{1,2,0:T(8,128)S(1)} fusion(bf16[16,8,128,128]{3,2,1,0:T(8,128)(2,1)} %bitcast.55, pred[16,8,128]{2,1,0:T(8,128)(4,1)S(1)} %iota_compare_fusion.7, bf16[9,16,32,128]{3,2,1,0:T(8,128)(2,1)} %get-tuple-element.164, s32[]{:T(128)S(6)} %copy.148), kind=kOutput, calls=%fused_computation.5.clone.1 | convolution fusion | flops 135262208 | bytes 4358148 | tf_op jit(solution)/shard_map/while/body/eval_jaxpr/mqd,mkpd->mqkp/dot_general | solution.py:34
  141.1 5.8 %all-to-all-start.1 = ((f32[16,9,8]{1,2,0:T(8,128)}), f32[16,9,8]{1,2,0:T(8,128)S(1)}, u32[]{:S(2)}, u32[]{:S(2)}) async-start(f32[16,9,8]{1,2,0:T(8,128)} %copy.120), calls=%async_computation.1 | async-start | bytes 131072 | tf_op jit(solution)/shard_map/all_to_all | solution.py:140
  147.0 6.9 %all-to-all-done.1 = f32[16,9,8]{1,2,0:T(8,128)S(1)} async-done(((f32[16,9,8]{1,2,0:T(8,128)}), f32[16,9,8]{1,2,0:T(8,128)S(1)}, u32[]{:S(2)}, u32[]{:S(2)}) %all-to-all-start.1) | async-done | bytes 4640 | tf_op jit(solution)/shard_map/all_to_all | solution.py:140
  154.1 4.5 %gather_fusion.3 = f32[768]{0:T(1024)S(1)} fusion(f32[1152]{0:T(1024)S(1)} %reshape.259, s32[1024]{0:T(1024)S(1)} %pad_clamp_fusion.1), kind=kCustom, calls=%fused_computation.3 | custom fusion | bytes 9216 | tf_op jit(solution)/shard_map/jit(_take)/gather | solution.py:144
  (199 shorter events, 60.1 us)
Async XLA Ops:
  0.0 1.7 %copy-start = (s32[512]{0:T(512)S(1)}, s32[512]{0:T(512)}, u32[]{:S(2)}) copy-start(s32[512]{0:T(512)} %param.15) | copy-start | bytes 6148
  1.7 5.5 %copy-start.3 = (bf16[32,32,128]{2,1,0:T(8,128)(2,1)S(1)}, bf16[32,32,128]{2,1,0:T(8,128)(2,1)}, u32[]{:S(2)}) copy-start(bf16[32,32,128]{2,1,0:T(8,128)(2,1)} %param.12) | copy-start | bytes 786436
  9.0 52.4 %all-to-all-start = ((bf16[16,9,32,128]{3,2,1,0:T(8,128)(2,1)}), bf16[16,9,32,128]{3,2,1,0:T(8,128)(2,1)}, u32[]{:S(2)}, u32[]{:S(2)}) async-start(bf16[16,9,32,128]{3,2,1,0:T(8,128)(2,1)} %copy.117), calls=%async_computation | async-start | bytes 2359296 | tf_op jit(solution)/shard_map/all_to_all | solution.py:131
  20.7 21.7 %collective-permute-start.14 = (bf16[1,9,8]{0,2,1:T(8,128)(2,1)}, bf16[1,9,8]{0,2,1:T(8,128)(2,1)S(1)}, u32[]{:S(2)}, u32[]{:S(2)}) collective-permute-start(bf16[1,9,8]{0,2,1:T(8,128)(2,1)} %get-tuple-element.82), channel_id=1, source_target_pairs={{0,1},{1,2},{2,3},{3,4},{4,5},{5,6},{6,7},{7,8},{8,9},{9,10},{10,1... | collective-permute-start | bytes 440 | tf_op jit(solution)/shard_map/ppermute | solution.py:19
  21.0 22.9 %collective-permute-start.13 = (bf16[1,9,8]{0,2,1:T(8,128)(2,1)}, bf16[1,9,8]{0,2,1:T(8,128)(2,1)S(1)}, u32[]{:S(2)}, u32[]{:S(2)}) collective-permute-start(bf16[1,9,8]{0,2,1:T(8,128)(2,1)} %get-tuple-element.83), channel_id=1, source_target_pairs={{0,2},{1,3},{2,4},{3,5},{4,6},{5,7},{6,8},{7,9},{8,10},{9,11},{10,... | collective-permute-start | bytes 440 | tf_op jit(solution)/shard_map/ppermute | solution.py:19
  22.6 25.3 %collective-permute-start.12 = (bf16[1,9,8]{0,2,1:T(8,128)(2,1)}, bf16[1,9,8]{0,2,1:T(8,128)(2,1)S(1)}, u32[]{:S(2)}, u32[]{:S(2)}) collective-permute-start(bf16[1,9,8]{0,2,1:T(8,128)(2,1)} %get-tuple-element.84), channel_id=1, source_target_pairs={{0,3},{1,4},{2,5},{3,6},{4,7},{5,8},{6,9},{7,10},{8,11},{9,12},{10... | collective-permute-start | bytes 440 | tf_op jit(solution)/shard_map/ppermute | solution.py:19
  24.9 23.7 %collective-permute-start.11 = (bf16[1,9,8]{0,2,1:T(8,128)(2,1)}, bf16[1,9,8]{0,2,1:T(8,128)(2,1)S(1)}, u32[]{:S(2)}, u32[]{:S(2)}) collective-permute-start(bf16[1,9,8]{0,2,1:T(8,128)(2,1)} %get-tuple-element.85), channel_id=1, source_target_pairs={{0,4},{1,5},{2,6},{3,7},{4,8},{5,9},{6,10},{7,11},{8,12},{9,13},{1... | collective-permute-start | bytes 440 | tf_op jit(solution)/shard_map/ppermute | solution.py:19
  26.4 24.4 %collective-permute-start.10 = (bf16[1,9,8]{0,2,1:T(8,128)(2,1)}, bf16[1,9,8]{0,2,1:T(8,128)(2,1)S(1)}, u32[]{:S(2)}, u32[]{:S(2)}) collective-permute-start(bf16[1,9,8]{0,2,1:T(8,128)(2,1)} %get-tuple-element.86), channel_id=1, source_target_pairs={{0,5},{1,6},{2,7},{3,8},{4,9},{5,10},{6,11},{7,12},{8,13},{9,14},{... | collective-permute-start | bytes 440 | tf_op jit(solution)/shard_map/ppermute | solution.py:19
  26.9 5.4 %copy-start.4 = (f32[4]{0:T(128)S(1)}, f32[4]{0:T(128)}, u32[]{:S(2)}) copy-start(f32[4]{0:T(128)} %param.19) | copy-start | bytes 52
  26.9 6.1 %copy-start.2 = (s32[32,128,128]{2,1,0:T(8,128)S(1)}, s32[32,128,128]{2,1,0:T(8,128)}, u32[]{:S(2)}) copy-start(s32[32,128,128]{2,1,0:T(8,128)} %param.17) | copy-start | bytes 6291460
  37.7 23.7 %copy-start.1 = (s32[32]{0:T(128)S(1)}, s32[32]{0:T(128)}, u32[]{:S(2)}) copy-start(s32[32]{0:T(128)} %param.18) | copy-start | bytes 388
  42.4 11.0 %collective-permute-start.9 = (bf16[1,9,8]{0,2,1:T(8,128)(2,1)}, bf16[1,9,8]{0,2,1:T(8,128)(2,1)S(1)}, u32[]{:S(2)}, u32[]{:S(2)}) collective-permute-start(bf16[1,9,8]{0,2,1:T(8,128)(2,1)} %get-tuple-element.87), channel_id=1, source_target_pairs={{0,6},{1,7},{2,8},{3,9},{4,10},{5,11},{6,12},{7,13},{8,14},{9,15},... | collective-permute-start | bytes 440 | tf_op jit(solution)/shard_map/ppermute | solution.py:19
  43.9 10.3 %collective-permute-start.8 = (bf16[1,9,8]{0,2,1:T(8,128)(2,1)S(1)}, bf16[1,9,8]{0,2,1:T(8,128)(2,1)S(1)}, u32[]{:S(2)}, u32[]{:S(2)}) collective-permute-start(bf16[1,9,8]{0,2,1:T(8,128)(2,1)S(1)} %get-tuple-element.88), channel_id=1, source_target_pairs={{0,7},{1,8},{2,9},{3,10},{4,11},{5,12},{6,13},{7,14},{8,15},{9,0},... | collective-permute-start | bytes 440 | tf_op jit(solution)/shard_map/ppermute | solution.py:19
  48.0 8.0 %collective-permute-start.7 = (bf16[1,9,8]{0,2,1:T(8,128)(2,1)S(1)}, bf16[1,9,8]{0,2,1:T(8,128)(2,1)S(1)}, u32[]{:S(2)}, u32[]{:S(2)}) collective-permute-start(bf16[1,9,8]{0,2,1:T(8,128)(2,1)S(1)} %get-tuple-element.89), channel_id=1, source_target_pairs={{0,8},{1,9},{2,10},{3,11},{4,12},{5,13},{6,14},{7,15},{8,0},{9,1},... | collective-permute-start | bytes 440 | tf_op jit(solution)/shard_map/ppermute | solution.py:19
  48.5 7.5 %collective-permute-start.6 = (bf16[1,9,8]{0,2,1:T(8,128)(2,1)S(1)}, bf16[1,9,8]{0,2,1:T(8,128)(2,1)S(1)}, u32[]{:S(2)}, u32[]{:S(2)}) collective-permute-start(bf16[1,9,8]{0,2,1:T(8,128)(2,1)S(1)} %get-tuple-element.90), channel_id=1, source_target_pairs={{0,9},{1,10},{2,11},{3,12},{4,13},{5,14},{6,15},{7,0},{8,1},{9,2},... | collective-permute-start | bytes 440 | tf_op jit(solution)/shard_map/ppermute | solution.py:19
  50.8 6.4 %collective-permute-start.5 = (bf16[1,9,8]{0,2,1:T(8,128)(2,1)S(1)}, bf16[1,9,8]{0,2,1:T(8,128)(2,1)S(1)}, u32[]{:S(2)}, u32[]{:S(2)}) collective-permute-start(bf16[1,9,8]{0,2,1:T(8,128)(2,1)S(1)} %get-tuple-element.91), channel_id=1, source_target_pairs={{0,10},{1,11},{2,12},{3,13},{4,14},{5,15},{6,0},{7,1},{8,2},{9,3},... | collective-permute-start | bytes 440 | tf_op jit(solution)/shard_map/ppermute | solution.py:19
  53.4 6.1 %collective-permute-start.4 = (bf16[1,9,8]{0,2,1:T(8,128)(2,1)S(1)}, bf16[1,9,8]{0,2,1:T(8,128)(2,1)S(1)}, u32[]{:S(2)}, u32[]{:S(2)}) collective-permute-start(bf16[1,9,8]{0,2,1:T(8,128)(2,1)S(1)} %get-tuple-element.92), channel_id=1, source_target_pairs={{0,11},{1,12},{2,13},{3,14},{4,15},{5,0},{6,1},{7,2},{8,3},{9,4},{... | collective-permute-start | bytes 440 | tf_op jit(solution)/shard_map/ppermute | solution.py:19
  54.2 5.3 %collective-permute-start.3 = (bf16[1,9,8]{0,2,1:T(8,128)(2,1)S(1)}, bf16[1,9,8]{0,2,1:T(8,128)(2,1)S(1)}, u32[]{:S(2)}, u32[]{:S(2)}) collective-permute-start(bf16[1,9,8]{0,2,1:T(8,128)(2,1)S(1)} %get-tuple-element.93), channel_id=1, source_target_pairs={{0,12},{1,13},{2,14},{3,15},{4,0},{5,1},{6,2},{7,3},{8,4},{9,5},{1... | collective-permute-start | bytes 440 | tf_op jit(solution)/shard_map/ppermute | solution.py:19
  56.0 3.5 %collective-permute-start.2 = (bf16[1,9,8]{0,2,1:T(8,128)(2,1)S(1)}, bf16[1,9,8]{0,2,1:T(8,128)(2,1)S(1)}, u32[]{:S(2)}, u32[]{:S(2)}) collective-permute-start(bf16[1,9,8]{0,2,1:T(8,128)(2,1)S(1)} %get-tuple-element.94), channel_id=1, source_target_pairs={{0,13},{1,14},{2,15},{3,0},{4,1},{5,2},{6,3},{7,4},{8,5},{9,6},{10... | collective-permute-start | bytes 440 | tf_op jit(solution)/shard_map/ppermute | solution.py:19
  56.0 3.8 %collective-permute-start.1 = (bf16[1,9,8]{0,2,1:T(8,128)(2,1)S(1)}, bf16[1,9,8]{0,2,1:T(8,128)(2,1)S(1)}, u32[]{:S(2)}, u32[]{:S(2)}) collective-permute-start(bf16[1,9,8]{0,2,1:T(8,128)(2,1)S(1)} %get-tuple-element.95), channel_id=1, source_target_pairs={{0,14},{1,15},{2,0},{3,1},{4,2},{5,3},{6,4},{7,5},{8,6},{9,7},{10,... | collective-permute-start | bytes 440 | tf_op jit(solution)/shard_map/ppermute | solution.py:19
  57.2 3.8 %collective-permute-start = (bf16[1,9,8]{0,2,1:T(8,128)(2,1)S(1)}, bf16[1,9,8]{0,2,1:T(8,128)(2,1)S(1)}, u32[]{:S(2)}, u32[]{:S(2)}) collective-permute-start(bf16[1,9,8]{0,2,1:T(8,128)(2,1)S(1)} %get-tuple-element.96), channel_id=1, source_target_pairs={{0,15},{1,0},{2,1},{3,2},{4,3},{5,4},{6,5},{7,6},{8,7},{9,8},{10,9... | collective-permute-start | bytes 440 | tf_op jit(solution)/shard_map/ppermute | solution.py:19
  141.1 12.7 %all-to-all-start.1 = ((f32[16,9,8]{1,2,0:T(8,128)}), f32[16,9,8]{1,2,0:T(8,128)S(1)}, u32[]{:S(2)}, u32[]{:S(2)}) async-start(f32[16,9,8]{1,2,0:T(8,128)} %copy.120), calls=%async_computation.1 | async-start | bytes 131072 | tf_op jit(solution)/shard_map/all_to_all | solution.py:140
  154.1 4.6 %copy-start.5 = (s32[32]{0:T(128)S(1)}, s32[32]{0:T(128)}, u32[]{:S(2)}) copy-start(s32[32]{0:T(128)} %param.14) | copy-start | bytes 388
